TPU v7x, 32 devices: a whole 2x2x4 slice. The times are simulated.
32 devices in a mesh: seq: 4 (over y, x), fsdp: 8 (over z, core).
Axes of the slice: x: 2, y: 2, z: 4, core: 2. Of those that a mesh axis runs over, the one named last changes fastest.
Arguments:
- tokens: bfloat16 [8, 1024, 1536], P('fsdp', 'seq'), may hold values from -6 to 6
- mixing_weight: bfloat16 [1536, 2560], P(('seq', 'fsdp')), may hold values from -0.21875 to 0.21875
- output_weight: bfloat16 [1536, 1536], P(('seq', 'fsdp')), may hold values from -0.625 to 0.625
- norm_gains: bfloat16 [1536, 2], P(('seq', 'fsdp')), may hold values from 0.099609375 to 1.8984375
- expert_gate: bfloat16 [1536, 40, 512], P('fsdp', 'seq'), may hold values from -0.15625 to 0.15625
- expert_up: bfloat16 [1536, 40, 512], P('fsdp', 'seq'), may hold values from -0.15625 to 0.15625
- expert_down: bfloat16 [1536, 40, 512], P('fsdp', 'seq'), may hold values from -1.25 to 1.25
- gate_logits: float32 [8, 1024, 8], P('fsdp'), may hold values from -3 to 3
- routes: int32 [8, 1024, 8], P('fsdp'), may hold values from 0 to 39, all different within a row
- fill_order: int32 [8, 1024], P('fsdp'), may hold values from 0 to 1023, each once within a row
- cotangent: bfloat16 [8, 1024, 1536], P('fsdp', 'seq'), may hold values from -6 to 6
Outputs:
- layer_output: bfloat16 [8, 1024, 1536], P('fsdp', 'seq')
- tokens_gradient: float32 [8, 1024, 1536], P('fsdp', 'seq')
- mixing_gradient: float32 [1536, 2560], P(('seq', 'fsdp'))
- output_gradient: float32 [1536, 1536], P(('seq', 'fsdp'))
- gains_gradient: float32 [1536, 2], P(('seq', 'fsdp'))
- gate_gradient: float32 [1536, 40, 512], P('fsdp', 'seq')
- up_gradient: float32 [1536, 40, 512], P('fsdp', 'seq')
- down_gradient: float32 [1536, 40, 512], P('fsdp', 'seq')
- logits_gradient: float32 [8, 1024, 8], P('fsdp', 'seq')
Inputs may be any that keep to these rules, and one draw needn't show every extreme that they name: `routes`: each token names 8 different experts. `fill_order`: each sequence's row holds each token index of that sequence once.
All inputs are finite; a program needn't handle non-finite values.
Results may differ from a plain program's by a relative error of at most 0.017.
The roundings to bfloat16 on the way count: a program that leaves them out, or rounds other values in their place, can miss the bound.
Values may be sent and summed in bfloat16 or wider, within the bound.
A program may use at most 256 MiB of HBM per device.

v0:
```python
import math
import jax
import jax.numpy as jnp
from jax import lax
from jax.sharding import PartitionSpec as P

D = 1536
HEADS = 24
KV_HEADS = 8
HEAD_DIM = 64
FF = 512
EXPERTS = 40
TOP = 8
QBLK = 512
epsilon = 1e-05
rope_base = 10000.0


def norm_apply(values, gain_row):
    return (
        values * lax.rsqrt(jnp.mean(values * values, axis=-1, keepdims=True) + epsilon) * gain_row
    )


def rotary_tables(positions):
    half_width = HEAD_DIM // 2
    frequency = rope_base ** (-2.0 * jnp.arange(half_width, dtype=jnp.float32) / HEAD_DIM)
    angles = positions.astype(jnp.float32)[:, None] * frequency[None, :]
    cos_table = jnp.cos(angles)
    sin_table = jnp.sin(angles)
    return (jnp.concatenate([cos_table, cos_table], 1), jnp.concatenate([sin_table, sin_table], 1))


def rotate(values, cos_table, sin_table):
    half_width = values.shape[-1] // 2
    turned = jnp.concatenate([-values[..., half_width:], values[..., :half_width]], -1)
    return values * cos_table[:, None, :] + turned * sin_table[:, None, :]


def softmax_last(logit_rows):
    row_max = jnp.max(logit_rows, axis=-1, keepdims=True)
    exponent = jnp.exp(logit_rows - row_max)
    return exponent / jnp.sum(exponent, axis=-1, keepdims=True)


def build_slots(route_rows, order_rows, expert_ids, capacity):
    length = route_rows.shape[0]
    chosen = route_rows[:, :, None] == expert_ids[None, None, :]
    hit_count = jnp.sum(chosen.astype(jnp.int32), axis=1)
    ordered = hit_count[order_rows]
    before = jnp.cumsum(ordered, axis=0) - ordered
    slot_rank = jnp.zeros_like(before).at[order_rows].set(before)
    kept_mask = (hit_count > 0) & (slot_rank < capacity)
    slot_place = jnp.where(kept_mask, slot_rank, capacity)
    expert_cols = jnp.broadcast_to(
        jnp.arange(expert_ids.shape[0], dtype=jnp.int32)[None, :], slot_place.shape
    )
    token_ids = jnp.broadcast_to(jnp.arange(length, dtype=jnp.int32)[:, None], slot_place.shape)
    table_full = jnp.full((expert_ids.shape[0], capacity + 1), length, jnp.int32)
    table_full = table_full.at[expert_cols, slot_place].set(token_ids)
    return (chosen, table_full[:, :capacity])


def local(
    tokens,
    mixing_weight,
    output_weight,
    norm_gains,
    expert_gate,
    expert_up,
    expert_down,
    gate_logits,
    routes,
    fill_order,
    cotangent,
):
    single = jnp.float32
    narrow = jnp.bfloat16
    groups = lax.axis_size("seq")
    column = lax.axis_index("seq")
    tok_rows = tokens.shape[1]
    seq_len = tok_rows * groups
    capacity = (seq_len * TOP + EXPERTS - 1) // EXPERTS
    local_count = expert_gate.shape[1]
    query_width = HEADS * HEAD_DIM
    key_width = KV_HEADS * HEAD_DIM
    mixing_width = query_width + 2 * key_width
    score_scale = 1.0 / math.sqrt(HEAD_DIM)
    group_size = HEADS // KV_HEADS
    inputs = tokens[0].astype(single)
    mixing_full, exit_full, gains_full = (
        lax.all_gather(mixing_weight, ("seq", "fsdp"), axis=0, tiled=True),
        lax.all_gather(output_weight, ("seq", "fsdp"), axis=0, tiled=True),
        lax.all_gather(norm_gains, ("seq", "fsdp"), axis=0, tiled=True),
    )
    gains_float = gains_full.astype(single)
    normed = norm_apply(inputs, gains_float[:, 0])
    normed_low = normed.astype(narrow)
    projected = jnp.dot(normed_low, mixing_full, preferred_element_type=single)
    positions = column * tok_rows + jnp.arange(tok_rows, dtype=jnp.int32)
    cos_table, sin_table = rotary_tables(positions)
    query_raw = projected[:, :query_width].reshape(tok_rows, HEADS, HEAD_DIM)
    key_raw = projected[:, query_width : query_width + key_width].reshape(
        tok_rows, KV_HEADS, HEAD_DIM
    )
    query_send = (
        rotate(query_raw, cos_table, sin_table).reshape(tok_rows, query_width).astype(narrow)
    )
    key_send = rotate(key_raw, cos_table, sin_table).reshape(tok_rows, key_width).astype(narrow)
    value_send = projected[:, query_width + key_width :].astype(narrow)
    query_heads, key_heads, value_heads = (
        lax.all_to_all(query_send, "seq", split_axis=1, concat_axis=0, tiled=True),
        lax.all_to_all(key_send, "seq", split_axis=1, concat_axis=0, tiled=True),
        lax.all_to_all(value_send, "seq", split_axis=1, concat_axis=0, tiled=True),
    )
    local_kv = key_heads.shape[1] // HEAD_DIM
    blocks = seq_len // QBLK
    query_blocks = query_heads.reshape(blocks, QBLK, local_kv, group_size, HEAD_DIM)
    key_heads = key_heads.reshape(seq_len, local_kv, HEAD_DIM)
    value_heads = value_heads.reshape(seq_len, local_kv, HEAD_DIM)
    starts = jnp.arange(blocks, dtype=jnp.int32) * QBLK
    key_pos = jnp.arange(seq_len, dtype=jnp.int32)

    def block_scores(row_block, first_row):
        scores = (
            jnp.einsum("bkgd,tkd->kgbt", row_block, key_heads, preferred_element_type=single)
            * score_scale
        )
        allowed = (first_row + jnp.arange(QBLK, dtype=jnp.int32))[:, None] >= key_pos[None, :]
        return jnp.where(allowed, scores, -jnp.inf)

    def attend(block_items):
        row_block, first_row = block_items
        scores = block_scores(row_block, first_row)
        row_max = jnp.max(scores, axis=-1, keepdims=True)
        exponent = jnp.exp(scores - row_max)
        row_total = jnp.sum(exponent, axis=-1, keepdims=True)
        soft_weights = (exponent / row_total).astype(narrow)
        attended = jnp.einsum(
            "kgbt,tkd->bkgd", soft_weights, value_heads, preferred_element_type=single
        )
        return (attended.astype(narrow), (row_max + jnp.log(row_total))[..., 0])

    attended_blocks, log_totals = lax.map(attend, (query_blocks, starts))
    attended_heads = attended_blocks.reshape(seq_len, -1)
    attn_rows = lax.all_to_all(attended_heads, "seq", split_axis=0, concat_axis=1, tiled=True)
    attn_out = lax.dot_general(
        attn_rows, exit_full, (((1,), (1,)), ((), ())), preferred_element_type=single
    )
    hidden = inputs + attn_out
    normed_two = norm_apply(hidden, gains_float[:, 1])
    normed_two_low = normed_two.astype(narrow)
    seq_rows = lax.all_gather(normed_two_low, "seq", axis=0, tiled=True)
    expert_ids = column * local_count + jnp.arange(local_count, dtype=jnp.int32)
    gating = softmax_last(gate_logits[0])
    chosen, slot_table = build_slots(routes[0], fill_order[0], expert_ids, capacity)
    chosen_float = chosen.astype(single)
    token_weight = jnp.sum(gating[:, :, None] * chosen_float, axis=1)
    padded_weight = jnp.concatenate([token_weight, jnp.zeros((1, local_count), single)], 0)
    expert_cols = jnp.arange(local_count, dtype=jnp.int32)[:, None]
    slot_weight = padded_weight[slot_table, expert_cols]
    padded_rows = jnp.concatenate([seq_rows, jnp.zeros((1, D), narrow)], 0)
    slot_rows = padded_rows[slot_table]
    gate_full, up_full, down_full = (
        lax.all_gather(expert_gate, "fsdp", axis=0, tiled=True),
        lax.all_gather(expert_up, "fsdp", axis=0, tiled=True),
        lax.all_gather(expert_down, "fsdp", axis=0, tiled=True),
    )
    gate_pre = jnp.einsum("ecd,def->ecf", slot_rows, gate_full, preferred_element_type=single)
    up_pre = jnp.einsum("ecd,def->ecf", slot_rows, up_full, preferred_element_type=single)
    sigmoid_gate = jax.nn.sigmoid(gate_pre)
    mid_low = (gate_pre * sigmoid_gate * up_pre).astype(narrow)
    expert_out = jnp.einsum("ecf,def->ecd", mid_low, down_full, preferred_element_type=single)
    partial_sum = (
        jnp.zeros((seq_len + 1, D), single)
        .at[slot_table]
        .add(expert_out * slot_weight[:, :, None])[:seq_len]
    )
    moe_rows = lax.psum_scatter(
        partial_sum.astype(jnp.bfloat16), "seq", scatter_dimension=0, tiled=True
    ).astype(jnp.float32)
    layer_output = (hidden + moe_rows).astype(narrow)[None]
    cot_rows = lax.all_gather(cotangent[0], "seq", axis=0, tiled=True)
    padded_cot = jnp.concatenate([cot_rows, jnp.zeros((1, D), narrow)], 0)
    slot_cot = padded_cot[slot_table].astype(single)
    slot_weight_grad = jnp.sum(slot_cot * expert_out, axis=-1)
    out_low = (slot_cot * slot_weight[:, :, None]).astype(narrow)
    gate_full, up_full, down_full = (
        lax.all_gather(expert_gate, "fsdp", axis=0, tiled=True),
        lax.all_gather(expert_up, "fsdp", axis=0, tiled=True),
        lax.all_gather(expert_down, "fsdp", axis=0, tiled=True),
    )
    mid_grad = jnp.einsum("ecd,def->ecf", out_low, down_full, preferred_element_type=single)
    gate_grad_low = (
        mid_grad * up_pre * sigmoid_gate * (1.0 + gate_pre * (1.0 - sigmoid_gate))
    ).astype(narrow)
    up_grad_low = (mid_grad * gate_pre * sigmoid_gate).astype(narrow)
    row_grad = jnp.einsum("ecf,def->ecd", gate_grad_low, gate_full, preferred_element_type=single)
    row_grad = row_grad + jnp.einsum(
        "ecf,def->ecd", up_grad_low, up_full, preferred_element_type=single
    )
    normed_two_part = jnp.zeros((seq_len + 1, D), single).at[slot_table].add(row_grad)[:seq_len]
    weight_grad_tok = (
        jnp.zeros((seq_len + 1, local_count), single)
        .at[slot_table, expert_cols]
        .add(slot_weight_grad)[:seq_len]
    )
    route_grad = jnp.sum(weight_grad_tok[:, None, :] * chosen_float, axis=-1)
    logit_part = gating * (route_grad - jnp.sum(gating * route_grad, axis=-1, keepdims=True))
    normed_two_grad, logits_rows = (
        lax.psum_scatter(normed_two_part, "seq", scatter_dimension=0, tiled=True),
        lax.psum_scatter(logit_part, "seq", scatter_dimension=0, tiled=True),
    )
    gate_term = jnp.einsum("ecd,ecf->def", slot_rows, gate_grad_low, preferred_element_type=single)
    up_term = jnp.einsum("ecd,ecf->def", slot_rows, up_grad_low, preferred_element_type=single)
    down_term = jnp.einsum("ecd,ecf->def", out_low, mid_low, preferred_element_type=single)
    expert_total = lax.psum_scatter(
        jnp.concatenate([gate_term, up_term, down_term], 2).astype(jnp.bfloat16),
        "fsdp",
        scatter_dimension=0,
        tiled=True,
    ).astype(jnp.float32)
    unused, norm_two_back = jax.vjp(norm_apply, hidden, gains_float[:, 1])
    hidden_part, gain_two_grad = norm_two_back(normed_two_grad)
    hidden_grad = cotangent[0].astype(single) + hidden_part
    attn_grad_low = hidden_grad.astype(narrow)
    attended_grad = jnp.dot(attn_grad_low, exit_full, preferred_element_type=single).astype(narrow)
    grads_heads = lax.all_to_all(attended_grad, "seq", split_axis=1, concat_axis=0, tiled=True)
    grad_blocks = grads_heads.reshape(blocks, QBLK, local_kv, group_size, HEAD_DIM)

    def attend_back(carried, block_items):
        keys_sum, values_sum = carried
        row_block, grad_block, block_log, first_row = block_items
        scores = block_scores(row_block, first_row)
        soft_float = jnp.exp(scores - block_log[..., None])
        soft_weights = soft_float.astype(narrow)
        values_sum = values_sum + jnp.einsum(
            "kgbt,bkgd->tkd", soft_weights, grad_block, preferred_element_type=single
        )
        soft_grad = jnp.einsum(
            "bkgd,tkd->kgbt", grad_block, value_heads, preferred_element_type=single
        )
        row_delta = jnp.sum(soft_float * soft_grad, axis=-1, keepdims=True)
        scores_grad = (soft_float * (soft_grad - row_delta)).astype(narrow)
        query_grad = (
            jnp.einsum("kgbt,tkd->bkgd", scores_grad, key_heads, preferred_element_type=single)
            * score_scale
        )
        keys_sum = (
            keys_sum
            + jnp.einsum("kgbt,bkgd->tkd", scores_grad, row_block, preferred_element_type=single)
            * score_scale
        )
        return ((keys_sum, values_sum), query_grad.astype(narrow))

    zero_heads = jnp.zeros((seq_len, local_kv, HEAD_DIM), single)
    (keys_sum, values_sum), query_grads = lax.scan(
        attend_back, (zero_heads, zero_heads), (query_blocks, grad_blocks, log_totals, starts)
    )
    query_send_grad = query_grads.reshape(seq_len, -1)
    key_send_grad = keys_sum.reshape(seq_len, -1).astype(narrow)
    value_send_grad = values_sum.reshape(seq_len, -1).astype(narrow)
    query_back, key_back, value_back = (
        lax.all_to_all(query_send_grad, "seq", split_axis=0, concat_axis=1, tiled=True),
        lax.all_to_all(key_send_grad, "seq", split_axis=0, concat_axis=1, tiled=True),
        lax.all_to_all(value_send_grad, "seq", split_axis=0, concat_axis=1, tiled=True),
    )

    def turn_rows(entries):
        return rotate(entries, cos_table, sin_table)

    unused, query_turn_back = jax.vjp(turn_rows, query_raw)
    unused, key_turn_back = jax.vjp(turn_rows, key_raw)
    query_raw_grad = query_turn_back(query_back.astype(single).reshape(tok_rows, HEADS, HEAD_DIM))[
        0
    ]
    key_raw_grad = key_turn_back(key_back.astype(single).reshape(tok_rows, KV_HEADS, HEAD_DIM))[0]
    projected_grad = jnp.concatenate(
        [
            query_raw_grad.reshape(tok_rows, query_width).astype(narrow),
            key_raw_grad.reshape(tok_rows, key_width).astype(narrow),
            value_back,
        ],
        1,
    )
    normed_grad = lax.dot_general(
        projected_grad, mixing_full, (((1,), (1,)), ((), ())), preferred_element_type=single
    )
    unused, norm_one_back = jax.vjp(norm_apply, inputs, gains_float[:, 0])
    input_part, gain_one_grad = norm_one_back(normed_grad)
    tokens_gradient = (hidden_grad + input_part)[None]
    gains_term = jnp.stack([gain_one_grad, gain_two_grad], 1)
    mixing_term = lax.dot_general(
        normed_low, projected_grad, (((0,), (0,)), ((), ())), preferred_element_type=single
    )
    output_term = lax.dot_general(
        attn_grad_low, attn_rows, (((0,), (0,)), ((), ())), preferred_element_type=single
    )
    attn_total = lax.psum_scatter(
        jnp.concatenate([mixing_term, output_term, gains_term], 1),
        ("seq", "fsdp"),
        scatter_dimension=0,
        tiled=True,
    )
    mixing_gradient = attn_total[:, :mixing_width]
    output_gradient = attn_total[:, mixing_width : mixing_width + query_width]
    gains_gradient = attn_total[:, mixing_width + query_width :]
    gate_gradient = expert_total[:, :, :FF]
    up_gradient = expert_total[:, :, FF : 2 * FF]
    down_gradient = expert_total[:, :, 2 * FF :]
    return (
        layer_output,
        tokens_gradient,
        mixing_gradient,
        output_gradient,
        gains_gradient,
        gate_gradient,
        up_gradient,
        down_gradient,
        logits_rows[None],
    )


def solution(mesh):
    in_specs = (
        P("fsdp", "seq", None),
        P(("seq", "fsdp"), None),
        P(("seq", "fsdp"), None),
        P(("seq", "fsdp"), None),
        P("fsdp", "seq", None),
        P("fsdp", "seq", None),
        P("fsdp", "seq", None),
        P("fsdp", None, None),
        P("fsdp", None, None),
        P("fsdp", None),
        P("fsdp", "seq", None),
    )
    out_specs = (
        P("fsdp", "seq", None),
        P("fsdp", "seq", None),
        P(("seq", "fsdp"), None),
        P(("seq", "fsdp"), None),
        P(("seq", "fsdp"), None),
        P("fsdp", "seq", None),
        P("fsdp", "seq", None),
        P("fsdp", "seq", None),
        P("fsdp", "seq", None),
    )
    return jax.shard_map(local, mesh=mesh, in_specs=in_specs, out_specs=out_specs, check_vma=False)
```

profile of v0, /device:TPU:0, one launch (start us, length us, event | category | flops | bytes accessed | tf_op | source)
XLA Modules:
  0.0 1854.2 jit_solution(63584453304176128)
XLA Ops:
  8.7 43.3 %all-gather.1 = bf16[32,48,2]{1,2,0:T(2,128)(2,1)S(1)} all-gather(bf16[1,48,2]{1,2,0:T(2,128)(2,1)} %bitcast.352), channel_id=1, replica_groups=mesh['seq'=4,'fsdp'=8] {'seq','fsdp'}, dimensions={0}, use_global_device_ids=true | all-gather | bytes 6336 | tf_op jit(solution)/shard_map/all_gather | solution.py:94
  57.3 32.0 %all-gather.10.cloned.1.call-done = bf16[1536,2560]{1,0:T(8,128)(2,1)} async-done(((bf16[48,2560]{1,0:T(8,128)(2,1)}), bf16[1536,2560]{1,0:T(8,128)(2,1)}) %all-gather.10.cloned.1.call-update) | async-done | bytes 7864336 | tf_op jit(solution)/shard_map/all_gather | solution.py:92
  131.2 12.9 all-to-all-done
  147.4 23.8 %while.28 = (s32[]{:T(128)}, bf16[2,512,2,3,64]{1,4,3,2,0:T(8,128)(2,1)S(1)}, f32[2,2,3,512]{3,2,1,0:T(4,128)S(1)}, s32[2]{0:T(128)S(1)}, bf16[2,512,2,3,64]{1,4...) while((s32[]{:T(128)}, ...), condition=%wide.region_4.5_spmd.clone, body=%wide.region_1.4_spmd.clone.sunk | while | flops 843773440 | bytes 41279608 | solution.py:144
  180.1 12.1 all-to-all-done.3
  213.5 37.9 %scatter_custom_fusion.3 = s32[2060]{0:T(1024)S(1)} fusion(s32[10240]{0:T(1024)S(1)} %reshape.356, s32[10240]{0:T(1024)S(1)} %reshape.358, s32[]{:T(128)} %constant.52.clone.1), kind=kCustom, calls=%fused_computation.179 | custom fusion | bytes 8244
  254.8 8.5 gather_fusion.3
  263.3 11.4 reshape.378
  276.8 8.5 gather_fusion.1
  285.3 8.8 reshape.311
  294.1 101.2 %all-gather.16.cloned.1.call-done = bf16[1536,10,512]{2,0,1:T(8,128)(2,1)} async-done(((bf16[192,10,512]{2,0,1:T(8,128)(2,1)}), bf16[1536,10,512]{2,0,1:T(8,128)(2,1)}) %all-gather.16.cloned.1.call-update) | async-done | bytes 15728656 | tf_op jit(solution)/shard_map/all_gather | solution.py:165
  395.3 13.3 fusion.103
  408.6 128.9 %all-gather.18.cloned.1.call-done = bf16[1536,10,512]{2,0,1:T(8,128)(2,1)} async-done(((bf16[192,10,512]{2,0,1:T(8,128)(2,1)}), bf16[1536,10,512]{2,0,1:T(8,128)(2,1)}) %all-gather.18.cloned.1.call-update) | async-done | bytes 15728656 | tf_op jit(solution)/shard_map/all_gather | solution.py:166
  537.5 15.1 multiply_convert_fusion.3
  552.6 127.2 %all-gather.20.cloned.1.call-done = bf16[1536,10,512]{2,0,1:T(8,128)(2,1)} async-done(((bf16[192,10,512]{2,0,1:T(8,128)(2,1)}), bf16[1536,10,512]{2,0,1:T(8,128)(2,1)}) %all-gather.20.cloned.1.call-update) | async-done | bytes 15728656 | tf_op jit(solution)/shard_map/all_gather | solution.py:167
  679.8 15.5 multiply_reduce_fusion
  695.4 16.0 scatter_custom_fusion.4
  712.6 19.8 %gather_fusion.2 = f32[2050]{0:T(1024)S(1)} fusion(f32[1025,10]{1,0:T(8,128)S(1)} %concatenate.44, s32[2050]{0:T(1024)S(1)} %reshape.318), kind=kCustom, calls=%fused_computation.2 | custom fusion | bytes 32800 | tf_op jit(solution)/shard_map/gather | solution.py:161
  732.5 15.0 multiply_convert_fusion.1
  747.5 12.8 fusion.104
  760.3 15.0 convolution_add_fusion
  775.3 12.5 reshape.352
  787.8 29.5 %scatter_custom_fusion.2 = f32[1025,1536]{1,0:T(8,128)} fusion(s32[2050]{0:T(1024)S(1)} %reshape.342, f32[2050,1536]{1,0:T(8,128)} %reshape.352, f32[]{:T(128)} %constant.30.clone.1), kind=kCustom, calls=%fused_computation.87 | custom fusion | flops 3148800 | bytes 6298112 | tf_op jit(solution)/shard_map/scatter-add | solution.py:202
  817.4 5.9 slice.109
  823.4 10.2 broadcast_multiply_fusion
  833.5 13.2 reshape.344
  846.7 29.4 %scatter_custom_fusion.1 = f32[1025,1536]{1,0:T(8,128)} fusion(s32[2050]{0:T(1024)S(1)} %reshape.342, f32[2050,1536]{1,0:T(8,128)} %reshape.344, f32[]{:T(128)} %constant.30.clone.1), kind=kCustom, calls=%fused_computation.89 | custom fusion | flops 3148800 | bytes 6298112 | tf_op jit(solution)/shard_map/scatter-add | solution.py:177
  881.1 10.8 reduce-scatter.10.cloned.1.call-done
  894.3 45.2 %reduce-scatter.8.cloned.1.call-done = bf16[256,1536]{1,0:T(8,128)(2,1)} async-done(((bf16[1024,1536]{1,0:T(8,128)(2,1)}), bf16[256,1536]{1,0:T(8,128)(2,1)}) %reduce-scatter.8.cloned.1.call-update) | async-done | bytes 786448 | tf_op jit(solution)/shard_map/reduce_scatter | solution.py:179
  952.3 11.0 all-to-all-done.4
  966.4 56.4 %while.29 = (s32[]{:T(128)}, f32[1024,2,64]{0,2,1:T(8,128)S(1)}, f32[1024,2,64]{0,2,1:T(8,128)}, bf16[2,512,2,3,64]{1,4,3,2,0:T(8,128)(2,1)}, bf16[2,512,2,3,64]...) while((s32[]{:T(128)}, f32[1024,2,64]{0,2,1:T(8,128)S(1)}, ...), condition=%wide.region_21.22_spmd.clone, body=%wide.region_19.21_spmd.clone.sunk | while | flops 2062022144 | bytes 184250800 | solution.py:257
  970.0 5.7 fusion.160
  985.0 6.6 fusion.163
  1013.2 6.6 fusion.163
  1027.4 6.7 fusion.75
  1042.8 9.5 all-to-all-done.5
  1061.1 7.9 fusion.72
  1069.0 6.8 fusion.65
  1076.1 27.7 %concatenate.48 = f32[1536,4098]{1,0:T(8,128)} concatenate(f32[1536,2560]{1,0:T(8,128)} %fusion.72, f32[1536,1536]{1,0:T(8,128)} %fusion.75, f32[1536,1]{1,0:T(8,128)S(1)} %stack.8, f32[1536,1]{1,0:T(8,128)S(1)} %copy-done.25), dimensions={1} | concatenate | bytes 50356224 | tf_op jit(solution)/shard_map/concatenate | solution.py:300
  1105.4 12.4 convert_bitcast_fusion.1
  1117.8 12.8 convert_bitcast_fusion.2
  1130.6 15.1 convert_bitcast_fusion
  1145.7 35.1 %pad_maximum_fusion = bf16[1536,10,1536]{0,2,1:T(8,128)(2,1)} fusion(bf16[1536,10,512]{0,2,1:T(8,128)(2,1)} %convert_bitcast_fusion, bf16[1536,10,512]{0,2,1:T(8,128)(2,1)} %convert_bitcast_fusion.1, bf16[1536,10,512]{0,2,1:T(8,128)(2,1)} %convert_bitcast_fusion.2), kind=kLoop, calls=%fused_computation.74 | loop fusion | flops 141557760 | bytes 94371840 | tf_op jit(solution)/shard_map/concatenate | solution.py:218
  1180.8 57.6 %copy.314 = bf16[1536,15360]{1,0:T(8,128)(2,1)} copy(bf16[1536,15360]{0,1:T(8,128)(2,1)} %bitcast.320) | data formatting | bytes 94371840
  1242.9 112.8 %reduce-scatter.12.cloned.1.call-done = f32[48,4098]{1,0:T(8,128)} async-done(((f32[1536,4098]{1,0:T(8,128)}), f32[48,4098]{1,0:T(8,128)}) %reduce-scatter.12.cloned.1.call-update) | async-done | bytes 786832 | tf_op jit(solution)/shard_map/reduce_scatter | solution.py:299
  1360.7 450.7 %reduce-scatter.16.cloned.1.call-done = bf16[192,15360]{1,0:T(8,128)(2,1)} async-done(((bf16[1536,15360]{1,0:T(8,128)(2,1)}), bf16[192,15360]{1,0:T(8,128)(2,1)}) %reduce-scatter.16.cloned.1.call-update) | async-done | bytes 5898256
  1811.3 9.7 copy.315
  1821.0 9.3 fusion.100
  (362 shorter events, 222.0 us)
Async XLA Ops:
  7.2 49.8 %copy-start.17 = (bf16[1,256,1536]{2,1,0:T(8,128)(2,1)S(1)}, bf16[1,256,1536]{2,1,0:T(8,128)(2,1)}, u32[]{:S(2)}) copy-start(bf16[1,256,1536]{2,1,0:T(8,128)(2,1)} %param.15) | copy-start | bytes 2359300
  7.2 82.1 %all-gather.10.cloned.1.call-start = ((), (), s32[]{:S(2)}) async-start(), calls=%async_computation.13 | async-start | bytes 8110080 | tf_op jit(solution)/shard_map/all_gather | solution.py:92
  7.9 172.2 %all-gather.12.cloned.1.call-start = ((), (), s32[]{:S(2)}) async-start(), calls=%async_computation.14 | async-start | bytes 4866048 | tf_op jit(solution)/shard_map/all_gather | solution.py:93
  52.3 42.5 %copy-start.26 = (f32[256,64]{0,1:T(8,128)}, f32[256,64]{0,1:T(8,128)S(1)}, u32[]{:S(2)}) copy-start(f32[256,64]{0,1:T(8,128)S(1)} %get-tuple-element.430) | copy-start | bytes 196612
  52.3 53.7 %copy-start.28 = (f32[256,64]{0,1:T(8,128)}, f32[256,64]{0,1:T(8,128)S(1)}, u32[]{:S(2)}) copy-start(f32[256,64]{0,1:T(8,128)S(1)} %get-tuple-element.431) | copy-start | bytes 196612
  57.0 37.8 %copy-start.36 = (f32[1536]{0:T(1024)}, f32[1536]{0:T(1024)S(1)}, u32[]{:S(2)}) copy-start(f32[1536]{0:T(1024)S(1)} %get-tuple-element.365) | copy-start | bytes 18436
  57.0 140.0 %copy-start.42 = (f32[1536]{0:T(1024)}, f32[1536]{0:T(1024)S(1)}, u32[]{:S(2)}) copy-start(f32[1536]{0:T(1024)S(1)} %get-tuple-element.364) | copy-start | bytes 18436
  57.2 37.6 %copy-start.54 = (f32[256]{0:T(256)}, f32[256]{0:T(256)S(1)}, u32[]{:S(2)}) copy-start(f32[256]{0:T(256)S(1)} %fusion.69) | copy-start | bytes 3076
  57.2 37.6 %copy-start.50 = (f32[256]{0:T(256)}, f32[256]{0:T(256)S(1)}, u32[]{:S(2)}) copy-start(f32[256]{0:T(256)S(1)} %fusion.95) | copy-start | bytes 3076
  108.1 9.4 all-to-all-start.1
  117.5 8.8 all-to-all-start.2
  126.2 17.9 all-to-all-start
  129.7 122.4 %all-gather.22.cloned.1.call-start = ((), (), s32[]{:S(2)}) async-start(), calls=%async_computation.23 | async-start | bytes 3932160 | tf_op jit(solution)/shard_map/all_gather | solution.py:183
  171.2 25.2 %copy-start.1 = (bf16[1024,2,64]{0,2,1:T(8,128)(2,1)}, bf16[1024,2,64]{0,2,1:T(8,128)(2,1)S(1)}, u32[]{:S(2)}) copy-start(bf16[1024,2,64]{0,2,1:T(8,128)(2,1)S(1)} %get-tuple-element.621) | copy-start | bytes 786436
  171.2 25.2 %copy-start.3 = (bf16[2,512,2,3,64]{1,4,3,2,0:T(8,128)(2,1)}, bf16[2,512,2,3,64]{1,4,3,2,0:T(8,128)(2,1)S(1)}, u32[]{:S(2)}) copy-start(bf16[2,512,2,3,64]{1,4,3,2,0:T(8,128)(2,1)S(1)} %get-tuple-element.622) | copy-start | bytes 2359300
  171.2 25.2 %copy-start.16 = (bf16[1024,2,64]{0,2,1:T(8,128)(2,1)}, bf16[1024,2,64]{0,2,1:T(8,128)(2,1)S(1)}, u32[]{:S(2)}) copy-start(bf16[1024,2,64]{0,2,1:T(8,128)(2,1)S(1)} %get-tuple-element.629) | copy-start | bytes 786436
  171.2 25.2 %copy-start.38 = (f32[2,2,3,512]{3,2,1,0:T(4,128)}, f32[2,2,3,512]{3,2,1,0:T(4,128)S(1)}, u32[]{:S(2)}) copy-start(f32[2,2,3,512]{3,2,1,0:T(4,128)S(1)} %get-tuple-element.575) | copy-start | bytes 73732
  171.2 25.2 %copy-start.63 = (s32[2]{0:T(128)}, s32[2]{0:T(128)S(1)}, u32[]{:S(2)}) copy-start(s32[2]{0:T(128)S(1)} %get-tuple-element.663) | copy-start | bytes 28
  176.5 15.7 all-to-all-start.3
  180.0 94.7 %all-gather.14.cloned.1.call-start = ((), (), s32[]{:S(2)}) async-start(), calls=%async_computation.15 | async-start | bytes 3932160 | tf_op jit(solution)/shard_map/all_gather | solution.py:153
  198.7 196.6 %all-gather.16.cloned.1.call-start = ((), (), s32[]{:S(2)}) async-start(), calls=%async_computation.16 | async-start | bytes 17694720 | tf_op jit(solution)/shard_map/all_gather | solution.py:165
  199.3 338.2 %all-gather.18.cloned.1.call-start = ((), (), s32[]{:S(2)}) async-start(), calls=%async_computation.17 | async-start | bytes 17694720 | tf_op jit(solution)/shard_map/all_gather | solution.py:166
  199.8 480.0 %all-gather.20.cloned.1.call-start = ((), (), s32[]{:S(2)}) async-start(), calls=%async_computation.18 | async-start | bytes 17694720 | tf_op jit(solution)/shard_map/all_gather | solution.py:167
  200.6 691.3 %reduce-scatter.10.cloned.1.call-start = ((), (), s32[]{:S(2)}) async-start(), calls=%async_computation.20 | async-start | bytes 7864320 | tf_op jit(solution)/shard_map/reduce_scatter | solution.py:211
  204.4 47.2 %copy-start.60 = (s32[2]{0:T(128)S(1)}, s32[2]{0:T(128)}, u32[]{:S(2)}) copy-start(s32[2]{0:T(128)} %constant.133) | copy-start | bytes 28
  204.4 47.3 %copy-start.59 = (s32[2]{0:T(128)S(1)}, s32[2]{0:T(128)}, u32[]{:S(2)}) copy-start(s32[2]{0:T(128)} %constant.136) | copy-start | bytes 28
  204.4 47.6 %copy-start.30 = (f32[1,1024,8]{1,2,0:T(8,128)S(1)}, f32[1,1024,8]{1,2,0:T(8,128)}, u32[]{:S(2)}) copy-start(f32[1,1024,8]{1,2,0:T(8,128)} %param.22) | copy-start | bytes 98308
  552.6 142.8 %copy-start.5 = (bf16[10,205,512]{2,1,0:T(8,128)(2,1)}, bf16[10,205,512]{2,1,0:T(8,128)(2,1)S(1)}, u32[]{:S(2)}) copy-start(bf16[10,205,512]{2,1,0:T(8,128)(2,1)S(1)} %get-tuple-element.425) | copy-start | bytes 6297604
  732.5 90.9 %copy-start.40 = (f32[10,205]{1,0:T(8,128)}, f32[10,205]{1,0:T(8,128)S(1)}, u32[]{:S(2)}) copy-start(f32[10,205]{1,0:T(8,128)S(1)} %reshape.321) | copy-start | bytes 24604
  823.3 116.2 %reduce-scatter.8.cloned.1.call-start = ((), (), s32[]{:S(2)}) async-start(), calls=%async_computation.19 | async-start | bytes 3932160 | tf_op jit(solution)/shard_map/reduce_scatter | solution.py:179
  876.2 15.8 copy-start.14
  876.2 15.8 copy-start.43
  876.2 15.8 copy-start.53
  881.1 13.2 copy-start.57
  881.1 58.4 %copy-start.20 = (bf16[1,256,1536]{2,1,0:T(8,128)(2,1)S(1)}, bf16[1,256,1536]{2,1,0:T(8,128)(2,1)}, u32[]{:S(2)}) copy-start(bf16[1,256,1536]{2,1,0:T(8,128)(2,1)} %param.25) | copy-start | bytes 2359300
  947.4 19.0 %copy-start.2 = (bf16[1024,2,64]{0,2,1:T(8,128)(2,1)S(1)}, bf16[1024,2,64]{0,2,1:T(8,128)(2,1)}, u32[]{:S(2)}) copy-start(bf16[1024,2,64]{0,2,1:T(8,128)(2,1)} %copy-done.1) | copy-start | bytes 786436
  947.4 19.0 %copy-start.4 = (bf16[2,512,2,3,64]{1,4,3,2,0:T(8,128)(2,1)S(1)}, bf16[2,512,2,3,64]{1,4,3,2,0:T(8,128)(2,1)}, u32[]{:S(2)}) copy-start(bf16[2,512,2,3,64]{1,4,3,2,0:T(8,128)(2,1)} %copy-done.3) | copy-start | bytes 2359300
  947.4 19.0 %copy-start.39 = (f32[2,2,3,512]{3,2,1,0:T(4,128)S(1)}, f32[2,2,3,512]{3,2,1,0:T(4,128)}, u32[]{:S(2)}) copy-start(f32[2,2,3,512]{3,2,1,0:T(4,128)} %copy-done.38) | copy-start | bytes 73732
  947.4 19.0 %copy-start.64 = (s32[2]{0:T(128)S(1)}, s32[2]{0:T(128)}, u32[]{:S(2)}) copy-start(s32[2]{0:T(128)} %copy-done.63) | copy-start | bytes 28
  948.6 14.7 all-to-all-start.4
  1023.7 14.7 all-to-all-start.6
  1038.4 14.0 all-to-all-start.5
  1052.4 8.8 all-to-all-start.7
  1055.8 300.0 %reduce-scatter.12.cloned.1.call-start = ((), (), s32[]{:S(2)}) async-start(), calls=%async_computation.21 | async-start | bytes 26763264 | tf_op jit(solution)/shard_map/reduce_scatter | solution.py:299
  1103.8 707.6 %reduce-scatter.16.cloned.1.call-start = ((), (), s32[]{:S(2)}) async-start(), calls=%async_computation.24 | async-start | bytes 53084160
  1117.7 12.8 copy-start.6
  1117.7 12.8 copy-start.41
  1238.4 608.5 %reduce-scatter.14.cloned.1.call-start = ((), (), s32[]{:S(2)}) async-start(), calls=%async_computation.22 | async-start | bytes 40960 | tf_op jit(solution)/shard_map/reduce_scatter | solution.py:212
  (48 other events, 239.1 us)
Sparse Core Ops, SparseCore 0:
  11.0 78.1 all-gather.9
  92.3 64.7 all-gather.11
  158.9 46.2 all-gather.21
  207.5 43.7 all-gather.13
  252.7 142.5 all-gather.15
  396.7 140.6 all-gather.17
  539.1 140.6 all-gather.19
  823.4 68.4 reduce-scatter.9
  895.5 43.9 reduce-scatter.7
  1103.9 251.8 reduce-scatter.11
  1358.1 453.1 reduce-scatter.15
  1814.5 21.9 reduce-scatter.13
where the time goes:
time: 1860 us; the launch traced here: 1850 us
  waiting for transfers between devices  1070 us (58%)
  local copies, waits for them, and re-layouts  315 us (17%)
  matrix products  216 us (12%)
  other arithmetic  165 us (9%)
  blocking collectives  43.3 us (2%)
  starting transfers between devices  29.8 us (2%)
    unnamed x13, waiting for transfers between devices  454 us
    unnamed x131, local copies, waits for them, and re-layouts  131 us
    all_gather x1, waiting for transfers between devices, local(): lax.all_gather(expert_up, 'fsdp', axis=0, tiled=True)  129 us
    all_gather x1, waiting for transfers between devices, local(): lax.all_gather(expert_down, 'fsdp', axis=0, tiled=True)  127 us
    reduce_scatter x1, waiting for transfers between devices, local(): lax.psum_scatter(jnp.concatenate([mixing_term, output_term, gains_term],...  113 us
    all_gather x1, waiting for transfers between devices, local(): lax.all_gather(expert_gate, 'fsdp', axis=0, tiled=True)  101 us
    reduce_scatter x1, waiting for transfers between devices, local(): lax.psum_scatter(partial_sum.astype(jnp.bfloat16), 'seq', scatter_dimensi...  45.2 us
    all_gather x1, blocking collectives, local(): lax.all_gather(norm_gains, ('seq', 'fsdp'), axis=0, tiled=True)  43.3 us
  transfers between devices with their start and end apart: 20, of which 15 were waited for; matrix products, arithmetic and copies ran while one was open for 23% of the time, Pallas kernels for 0%

commit v1 on v0

--- a/solution.py
+++ b/solution.py
@@ -14,6 +14,27 @@
 QBLK = 512
 epsilon = 1e-05
 rope_base = 10000.0
+
+
+def joined_along(blocks, dim):
+    dims = list(blocks.shape[1:])
+    dims[dim] *= blocks.shape[0]
+    return jnp.moveaxis(blocks, 0, dim).reshape(dims)
+
+
+def grow_blocks(array, axis):
+    size, mine = (lax.axis_size(axis), lax.axis_index(axis))
+    pieces, bit = (array[None], 1)
+    while bit < size:
+        other = lax.ppermute(pieces, axis, [(i, i ^ bit) for i in range(size)])
+        low = mine & bit == 0
+        pieces = jnp.concatenate([jnp.where(low, pieces, other), jnp.where(low, other, pieces)])
+        bit *= 2
+    return pieces
+
+
+def doubled_up(value, axis, dim):
+    return joined_along(grow_blocks(value, axis), dim)
 
 
 def norm_apply(values, gain_row):
@@ -162,7 +183,7 @@
     padded_rows = jnp.concatenate([seq_rows, jnp.zeros((1, D), narrow)], 0)
     slot_rows = padded_rows[slot_table]
     gate_full, up_full, down_full = (
-        lax.all_gather(expert_gate, "fsdp", axis=0, tiled=True),
+        doubled_up(expert_gate, "fsdp", 0),
         lax.all_gather(expert_up, "fsdp", axis=0, tiled=True),
         lax.all_gather(expert_down, "fsdp", axis=0, tiled=True),
     )

time: 1860 us -> 2250 us (1.21)
  waiting for transfers between devices: 1070 us -> 1420 us
  other arithmetic: 165 us -> 191 us
    ppermute x0 -> x3, waiting for transfers between devices: none -> 713 us  [grow_blocks(): other = lax.ppermute(pieces, axis, [(i, i ^ bit) for i in range(size)])]
    all_gather x1, waiting for transfers between devices: 129 us -> 0.01 us  [local(): lax.all_gather(expert_up, 'fsdp', axis=0, tiled=True)]
    all_gather x1, waiting for transfers between devices: 127 us -> 0.01 us  [local(): lax.all_gather(expert_down, 'fsdp', axis=0, tiled=True)]
    all_gather x1, waiting for transfers between devices: 101 us -> 0.01 us  [local(): lax.all_gather(expert_gate, 'fsdp', axis=0, tiled=True)]
    unnamed x131 -> x135, local copies, waits for them, and re-layouts: 131 us -> 133 us
  transfers between devices with their start and end apart: 20 -> 23, of which waited for: 15 -> 15; matrix products, arithmetic and copies ran while one was open for 23% -> 24% of each run, Pallas kernels for 0% -> 0%
where the time goes in v1:
time: 2250 us; the launch traced here: 2240 us
  waiting for transfers between devices  1420 us (63%)
  local copies, waits for them, and re-layouts  322 us (14%)
  matrix products  216 us (10%)
  other arithmetic  191 us (8%)
  blocking collectives  43.3 us (2%)
  starting transfers between devices  31.1 us (1%)
    ppermute x3, waiting for transfers between devices, grow_blocks(): other = lax.ppermute(pieces, axis, [(i, i ^ bit) for i in range(size)])  713 us
    unnamed x13, waiting for transfers between devices  454 us
    unnamed x135, local copies, waits for them, and re-layouts  133 us
    reduce_scatter x1, waiting for transfers between devices, local(): lax.psum_scatter(jnp.concatenate([mixing_term, output_term, gains_term],...  113 us
    reduce_scatter x1, waiting for transfers between devices, local(): lax.psum_scatter(partial_sum.astype(jnp.bfloat16), 'seq', scatter_dimensi...  45.2 us
  transfers between devices with their start and end apart: 23, of which 15 were waited for; matrix products, arithmetic and copies ran while one was open for 24% of the time, Pallas kernels for 0%

profile of v1, /device:TPU:0, one launch (start us, length us, event | category | flops | bytes accessed | tf_op | source)
XLA Modules:
  0.0 2244.1 jit_solution(1385385401761655952)
XLA Ops:
  8.7 43.3 %all-gather.1 = bf16[32,48,2]{1,2,0:T(2,128)(2,1)S(1)} all-gather(bf16[1,48,2]{1,2,0:T(2,128)(2,1)} %bitcast.358), channel_id=1, replica_groups=mesh['seq'=4,'fsdp'=8] {'seq','fsdp'}, dimensions={0}, use_global_device_ids=true | all-gather | bytes 6336 | tf_op jit(solution)/shard_map/all_gather | solution.py:115
  57.3 32.0 %all-gather.10.cloned.1.call-done = bf16[1536,2560]{1,0:T(8,128)(2,1)} async-done(((bf16[48,2560]{1,0:T(8,128)(2,1)}), bf16[1536,2560]{1,0:T(8,128)(2,1)}) %all-gather.10.cloned.1.call-update) | async-done | bytes 7864336 | tf_op jit(solution)/shard_map/all_gather | solution.py:113
  131.2 12.9 all-to-all-done
  147.5 23.8 %while.28 = (s32[]{:T(128)}, bf16[2,512,2,3,64]{1,4,3,2,0:T(8,128)(2,1)S(1)}, f32[2,2,3,512]{3,2,1,0:T(4,128)S(1)}, s32[2]{0:T(128)S(1)}, bf16[2,512,2,3,64]{1,4...) while((s32[]{:T(128)}, ...), condition=%wide.region_4.5_spmd.clone, body=%wide.region_1.4_spmd.clone.sunk | while | flops 843773440 | bytes 41279608 | solution.py:165
  180.2 12.3 all-to-all-done.3
  211.7 185.0 %collective-permute-done.1 = bf16[2,192,10,512]{3,1,2,0:T(8,128)(2,1)} collective-permute-done((bf16[2,192,10,512]{3,1,2,0:T(8,128)(2,1)}, bf16[2,192,10,512]{3,1,2,0:T(8,128)(2,1)}, u32[]{:S(2)}, u32[]{:S(2)}) %collective-permute-start.1) | collective-permute-done | bytes 3932192 | tf_op jit(solution)/shard_map/ppermute | solution.py:29
  401.9 7.2 pad_maximum_fusion.2
  422.1 38.1 %scatter_custom_fusion.3 = s32[2060]{0:T(1024)S(1)} fusion(s32[10240]{0:T(1024)S(1)} %reshape.360, s32[10240]{0:T(1024)S(1)} %reshape.362, s32[]{:T(128)} %constant.56.clone.1), kind=kCustom, calls=%fused_computation.188 | custom fusion | bytes 8244
  463.6 8.4 gather_fusion.3
  472.1 10.5 reshape.382
  482.6 523.5 %collective-permute-done.2 = bf16[4,192,10,512]{3,1,2,0:T(8,128)(2,1)} collective-permute-done((bf16[4,192,10,512]{3,1,2,0:T(8,128)(2,1)}, bf16[4,192,10,512]{3,1,2,0:T(8,128)(2,1)}, u32[]{:S(2)}, u32[]{:S(2)}) %collective-permute-start.2) | collective-permute-done | bytes 7864352 | tf_op jit(solution)/shard_map/ppermute | solution.py:29
  1006.1 6.1 broadcast_select_fusion.1
  1013.7 6.4 copy.293
  1022.2 8.5 gather_fusion.1
  1030.7 8.9 reshape.315
  1039.5 12.9 fusion.103
  1052.5 14.1 multiply_convert_fusion.3
  1066.6 16.3 multiply_reduce_fusion
  1083.0 16.0 scatter_custom_fusion.4
  1100.2 19.8 gather_fusion.2
  1120.1 15.9 multiply_convert_fusion.1
  1135.9 11.8 fusion.104
  1147.7 16.0 convolution_add_fusion
  1163.7 12.6 reshape.356
  1176.3 29.9 %scatter_custom_fusion.2 = f32[1025,1536]{1,0:T(8,128)} fusion(s32[2050]{0:T(1024)} %copy-done.50, f32[2050,1536]{1,0:T(8,128)} %reshape.356, f32[]{:T(128)} %constant.31.clone.1), kind=kCustom, calls=%fused_computation.94 | custom fusion | flops 3148800 | bytes 6298112 | tf_op jit(solution)/shard_map/scatter-add | solution.py:223
  1212.2 10.2 broadcast_multiply_fusion
  1222.4 12.8 reshape.348
  1235.2 29.5 %scatter_custom_fusion.1 = f32[1025,1536]{1,0:T(8,128)} fusion(s32[2050]{0:T(1024)} %copy-done.50, f32[2050,1536]{1,0:T(8,128)} %reshape.348, f32[]{:T(128)} %constant.31.clone.1), kind=kCustom, calls=%fused_computation.96 | custom fusion | flops 3148800 | bytes 6298112 | tf_op jit(solution)/shard_map/scatter-add | solution.py:198
  1269.6 11.9 reduce-scatter.10.cloned.1.call-done
  1283.9 45.2 %reduce-scatter.8.cloned.1.call-done = bf16[256,1536]{1,0:T(8,128)(2,1)} async-done(((bf16[1024,1536]{1,0:T(8,128)(2,1)}), bf16[256,1536]{1,0:T(8,128)(2,1)}) %reduce-scatter.8.cloned.1.call-update) | async-done | bytes 786448 | tf_op jit(solution)/shard_map/reduce_scatter | solution.py:200
  1341.9 11.0 all-to-all-done.4
  1355.9 56.5 %while.29 = (s32[]{:T(128)}, f32[1024,2,64]{0,2,1:T(8,128)S(1)}, f32[1024,2,64]{0,2,1:T(8,128)}, bf16[2,512,2,3,64]{1,4,3,2,0:T(8,128)(2,1)}, bf16[2,512,2,3,64]...) while((s32[]{:T(128)}, f32[1024,2,64]{0,2,1:T(8,128)S(1)}, ...), condition=%wide.region_21.22_spmd.clone, body=%wide.region_19.21_spmd.clone.sunk | while | flops 2062022144 | bytes 184250800 | solution.py:278
  1374.6 6.6 fusion.163
  1402.9 6.6 fusion.163
  1417.2 6.9 fusion.75
  1432.8 9.5 all-to-all-done.5
  1451.1 7.9 fusion.72
  1459.0 6.8 fusion.65
  1466.0 27.7 %concatenate.60 = f32[1536,4098]{1,0:T(8,128)} concatenate(f32[1536,2560]{1,0:T(8,128)} %fusion.72, f32[1536,1536]{1,0:T(8,128)} %fusion.75, f32[1536,1]{1,0:T(8,128)S(1)} %stack.8, f32[1536,1]{1,0:T(8,128)S(1)} %copy-done.26), dimensions={1} | concatenate | bytes 50356224 | tf_op jit(solution)/shard_map/concatenate | solution.py:321
  1495.3 12.3 convert_bitcast_fusion.1
  1507.6 12.8 convert_bitcast_fusion.2
  1520.4 15.1 convert_bitcast_fusion
  1535.5 35.6 %pad_maximum_fusion = bf16[1536,10,1536]{0,2,1:T(8,128)(2,1)} fusion(bf16[1536,10,512]{0,2,1:T(8,128)(2,1)} %convert_bitcast_fusion, bf16[1536,10,512]{0,2,1:T(8,128)(2,1)} %convert_bitcast_fusion.1, bf16[1536,10,512]{0,2,1:T(8,128)(2,1)} %convert_bitcast_fusion.2), kind=kLoop, calls=%fused_computation.74 | loop fusion | flops 141557760 | bytes 94371840 | tf_op jit(solution)/shard_map/concatenate | solution.py:239
  1571.1 57.5 %copy.322 = bf16[1536,15360]{1,0:T(8,128)(2,1)} copy(bf16[1536,15360]{0,1:T(8,128)(2,1)} %bitcast.324) | data formatting | bytes 94371840
  1633.1 112.8 %reduce-scatter.12.cloned.1.call-done = f32[48,4098]{1,0:T(8,128)} async-done(((f32[1536,4098]{1,0:T(8,128)}), f32[48,4098]{1,0:T(8,128)}) %reduce-scatter.12.cloned.1.call-update) | async-done | bytes 786832 | tf_op jit(solution)/shard_map/reduce_scatter | solution.py:320
  1750.8 450.7 %reduce-scatter.16.cloned.1.call-done = bf16[192,15360]{1,0:T(8,128)(2,1)} async-done(((bf16[1536,15360]{1,0:T(8,128)(2,1)}), bf16[192,15360]{1,0:T(8,128)(2,1)}) %reduce-scatter.16.cloned.1.call-update) | async-done | bytes 5898256
  2201.5 9.7 copy.323
  2211.2 9.3 fusion.100
  (379 shorter events, 251.5 us)
Async XLA Ops:
  7.2 49.8 %copy-start.17 = (bf16[1,256,1536]{2,1,0:T(8,128)(2,1)S(1)}, bf16[1,256,1536]{2,1,0:T(8,128)(2,1)}, u32[]{:S(2)}) copy-start(bf16[1,256,1536]{2,1,0:T(8,128)(2,1)} %param.15) | copy-start | bytes 2359300
  7.2 82.1 %all-gather.10.cloned.1.call-start = ((), (), s32[]{:S(2)}) async-start(), calls=%async_computation.13 | async-start | bytes 8110080 | tf_op jit(solution)/shard_map/all_gather | solution.py:113
  7.9 172.3 %all-gather.12.cloned.1.call-start = ((), (), s32[]{:S(2)}) async-start(), calls=%async_computation.14 | async-start | bytes 4866048 | tf_op jit(solution)/shard_map/all_gather | solution.py:114
  52.3 42.5 %copy-start.27 = (f32[256,64]{0,1:T(8,128)}, f32[256,64]{0,1:T(8,128)S(1)}, u32[]{:S(2)}) copy-start(f32[256,64]{0,1:T(8,128)S(1)} %get-tuple-element.436) | copy-start | bytes 196612
  52.3 53.6 %copy-start.29 = (f32[256,64]{0,1:T(8,128)}, f32[256,64]{0,1:T(8,128)S(1)}, u32[]{:S(2)}) copy-start(f32[256,64]{0,1:T(8,128)S(1)} %get-tuple-element.437) | copy-start | bytes 196612
  57.0 37.8 %copy-start.37 = (f32[1536]{0:T(1024)}, f32[1536]{0:T(1024)S(1)}, u32[]{:S(2)}) copy-start(f32[1536]{0:T(1024)S(1)} %get-tuple-element.365) | copy-start | bytes 18436
  57.0 140.2 %copy-start.43 = (f32[1536]{0:T(1024)}, f32[1536]{0:T(1024)S(1)}, u32[]{:S(2)}) copy-start(f32[1536]{0:T(1024)S(1)} %get-tuple-element.364) | copy-start | bytes 18436
  57.2 37.6 %copy-start.56 = (f32[256]{0:T(256)}, f32[256]{0:T(256)S(1)}, u32[]{:S(2)}) copy-start(f32[256]{0:T(256)S(1)} %fusion.69) | copy-start | bytes 3076
  57.2 37.6 %copy-start.52 = (f32[256]{0:T(256)}, f32[256]{0:T(256)S(1)}, u32[]{:S(2)}) copy-start(f32[256]{0:T(256)S(1)} %fusion.95) | copy-start | bytes 3076
  108.1 9.4 all-to-all-start.1
  117.5 8.8 all-to-all-start.2
  126.2 17.9 all-to-all-start
  129.7 331.3 %all-gather.22.cloned.1.call-start = ((), (), s32[]{:S(2)}) async-start(), calls=%async_computation.23 | async-start | bytes 3932160 | tf_op jit(solution)/shard_map/all_gather | solution.py:204
  171.2 25.4 %copy-start.1 = (bf16[1024,2,64]{0,2,1:T(8,128)(2,1)}, bf16[1024,2,64]{0,2,1:T(8,128)(2,1)S(1)}, u32[]{:S(2)}) copy-start(bf16[1024,2,64]{0,2,1:T(8,128)(2,1)S(1)} %get-tuple-element.626) | copy-start | bytes 786436
  171.3 25.4 %copy-start.3 = (bf16[2,512,2,3,64]{1,4,3,2,0:T(8,128)(2,1)}, bf16[2,512,2,3,64]{1,4,3,2,0:T(8,128)(2,1)S(1)}, u32[]{:S(2)}) copy-start(bf16[2,512,2,3,64]{1,4,3,2,0:T(8,128)(2,1)S(1)} %get-tuple-element.627) | copy-start | bytes 2359300
  171.3 25.4 %copy-start.16 = (bf16[1024,2,64]{0,2,1:T(8,128)(2,1)}, bf16[1024,2,64]{0,2,1:T(8,128)(2,1)S(1)}, u32[]{:S(2)}) copy-start(bf16[1024,2,64]{0,2,1:T(8,128)(2,1)S(1)} %get-tuple-element.635) | copy-start | bytes 786436
  171.3 25.4 %copy-start.39 = (f32[2,2,3,512]{3,2,1,0:T(4,128)}, f32[2,2,3,512]{3,2,1,0:T(4,128)S(1)}, u32[]{:S(2)}) copy-start(f32[2,2,3,512]{3,2,1,0:T(4,128)S(1)} %get-tuple-element.581) | copy-start | bytes 73732
  171.3 25.4 %copy-start.65 = (s32[2]{0:T(128)}, s32[2]{0:T(128)S(1)}, u32[]{:S(2)}) copy-start(s32[2]{0:T(128)S(1)} %get-tuple-element.671) | copy-start | bytes 28
  176.6 15.8 all-to-all-start.3
  180.1 839.9 %all-gather.14.cloned.1.call-start = ((), (), s32[]{:S(2)}) async-start(), calls=%async_computation.15 | async-start | bytes 3932160 | tf_op jit(solution)/shard_map/all_gather | solution.py:174
  198.9 853.6 %all-gather.16.cloned.1.call-start = ((), (), s32[]{:S(2)}) async-start(), calls=%async_computation.16 | async-start | bytes 17694720 | tf_op jit(solution)/shard_map/all_gather | solution.py:187
  199.5 867.1 %all-gather.18.cloned.1.call-start = ((), (), s32[]{:S(2)}) async-start(), calls=%async_computation.17 | async-start | bytes 17694720 | tf_op jit(solution)/shard_map/all_gather | solution.py:188
  200.1 935.9 %all-gather.20.cloned.1.call-start = ((), (), s32[]{:S(2)}) async-start(), calls=%async_computation.19 | async-start | bytes 17694720 | tf_op jit(solution)/shard_map/all_gather | solution.py:210
  200.8 1080.6 %reduce-scatter.10.cloned.1.call-start = ((), (), s32[]{:S(2)}) async-start(), calls=%async_computation.20 | async-start | bytes 7864320 | tf_op jit(solution)/shard_map/reduce_scatter | solution.py:232
  201.4 4.2 collective-permute-start
  211.5 185.1 %collective-permute-start.1 = (bf16[2,192,10,512]{3,1,2,0:T(8,128)(2,1)}, bf16[2,192,10,512]{3,1,2,0:T(8,128)(2,1)}, u32[]{:S(2)}, u32[]{:S(2)}) collective-permute-start(bf16[2,192,10,512]{3,1,2,0:T(8,128)(2,1)} %pad_maximum_fusion.3), channel_id=1, source_target_pairs={{0,2},{1,3},{2,0},{3,1},{4,6},{5,7},{6,4},{7,5},{8,10},{9,11},{10,... | collective-permute-start | bytes 11796488 | tf_op jit(solution)/shard_map/ppermute | solution.py:29
  409.1 597.0 %collective-permute-start.2 = (bf16[4,192,10,512]{3,1,2,0:T(8,128)(2,1)}, bf16[4,192,10,512]{3,1,2,0:T(8,128)(2,1)}, u32[]{:S(2)}, u32[]{:S(2)}) collective-permute-start(bf16[4,192,10,512]{3,1,2,0:T(8,128)(2,1)} %pad_maximum_fusion.2), channel_id=1, source_target_pairs={{0,4},{1,5},{2,6},{3,7},{4,0},{5,1},{6,2},{7,3},{8,12},{9,13},{10,... | collective-permute-start | bytes 23592968 | tf_op jit(solution)/shard_map/ppermute | solution.py:29
  413.1 47.4 %copy-start.62 = (s32[2]{0:T(128)S(1)}, s32[2]{0:T(128)}, u32[]{:S(2)}) copy-start(s32[2]{0:T(128)} %constant.142) | copy-start | bytes 28
  413.1 47.5 %copy-start.61 = (s32[2]{0:T(128)S(1)}, s32[2]{0:T(128)}, u32[]{:S(2)}) copy-start(s32[2]{0:T(128)} %constant.145) | copy-start | bytes 28
  413.1 47.8 %copy-start.31 = (f32[1,1024,8]{1,2,0:T(8,128)S(1)}, f32[1,1024,8]{1,2,0:T(8,128)}, u32[]{:S(2)}) copy-start(f32[1,1024,8]{1,2,0:T(8,128)} %param.22) | copy-start | bytes 98308
  1066.6 16.3 copy-start.5
  1120.1 92.1 %copy-start.41 = (f32[10,205]{1,0:T(8,128)}, f32[10,205]{1,0:T(8,128)S(1)}, u32[]{:S(2)}) copy-start(f32[10,205]{1,0:T(8,128)S(1)} %reshape.325) | copy-start | bytes 24604
  1212.1 116.9 %reduce-scatter.8.cloned.1.call-start = ((), (), s32[]{:S(2)}) async-start(), calls=%async_computation.18 | async-start | bytes 3932160 | tf_op jit(solution)/shard_map/reduce_scatter | solution.py:200
  1264.6 16.8 copy-start.14
  1264.6 16.8 copy-start.44
  1264.6 16.8 copy-start.55
  1269.6 59.5 %copy-start.21 = (bf16[1,256,1536]{2,1,0:T(8,128)(2,1)S(1)}, bf16[1,256,1536]{2,1,0:T(8,128)(2,1)}, u32[]{:S(2)}) copy-start(bf16[1,256,1536]{2,1,0:T(8,128)(2,1)} %param.25) | copy-start | bytes 2359300
  1336.9 19.0 copy-start.2
  1336.9 19.0 copy-start.4
  1337.0 19.0 copy-start.40
  1337.0 19.0 copy-start.66
  1338.1 14.8 all-to-all-start.4
  1413.4 15.0 all-to-all-start.6
  1428.3 14.0 all-to-all-start.5
  1442.3 8.8 all-to-all-start.7
  1445.7 300.2 %reduce-scatter.12.cloned.1.call-start = ((), (), s32[]{:S(2)}) async-start(), calls=%async_computation.21 | async-start | bytes 26763264 | tf_op jit(solution)/shard_map/reduce_scatter | solution.py:320
  1493.7 707.8 %reduce-scatter.16.cloned.1.call-start = ((), (), s32[]{:S(2)}) async-start(), calls=%async_computation.24 | async-start | bytes 53084160
  1628.7 608.4 %reduce-scatter.14.cloned.1.call-start = ((), (), s32[]{:S(2)}) async-start(), calls=%async_computation.22 | async-start | bytes 40960 | tf_op jit(solution)/shard_map/reduce_scatter | solution.py:233
  (53 other events, 280.4 us)
Sparse Core Ops, SparseCore 0:
  11.0 78.1 all-gather.9
  92.3 64.6 all-gather.11
  158.9 46.3 all-gather.21
  207.5 43.6 all-gather.13
  252.7 185.0 all-gather.15
  439.3 346.8 all-gather.17
  787.8 203.8 all-gather.19
  1212.3 69.1 reduce-scatter.9
  1285.0 43.9 reduce-scatter.7
  1493.8 252.0 reduce-scatter.11
  1748.3 453.1 reduce-scatter.15
  2204.7 21.8 reduce-scatter.13
